TPU v7x, 256 devices: a whole 4x4x8 slice. The times are simulated.
256 devices in a mesh: tx: 32 (over z, y), ty: 8 (over x, core).
Axes of the slice: x: 4, y: 4, z: 8, core: 2. Of those that a mesh axis runs over, the one named last changes fastest.
Arguments:
- probes: bfloat16 [4096, 1024, 128], P('tx', 'ty')
- filter_taps: float32 [2, 2, 33], replicated, may hold values from 0.05 to 1
- cluster_ranks: int32 [5, 32, 8], replicated, may hold values from 64 to 128
Outputs:
- leaf_basis: bfloat16 [4096, 1024, 128], P('tx', 'ty')
- transfers: float32 [32, 8, 4, 128, 128], P('tx', 'ty')
Inputs may be any that keep to these rules, and one draw needn't show every extreme that they name: `cluster_ranks`: only the entry of a cluster's first leaf (lowest row and column indices) is its rank at that level.
All inputs are finite; a program needn't handle non-finite values.
Results may differ from a plain program's by a relative error of at most 0.014.
The roundings to bfloat16 on the way count: a program that leaves them out, or rounds other values in their place, can miss the bound.
Values may be sent and summed in bfloat16 or wider, within the bound.
A program may use at most 128 MiB of HBM per device.

v0:
```python
import jax
import jax.numpy as jnp
from jax import lax
from jax.sharding import PartitionSpec as P


def extended(block, sides, width):
    for axis, dim in sides:
        count = lax.axis_size(axis)
        forward = [(i, i + 1) for i in range(count - 1)]
        backward = [(target, source) for source, target in forward]
        low = lax.ppermute(
            lax.slice_in_dim(block, block.shape[dim] - width, None, axis=dim), axis, forward
        )
        high = lax.ppermute(lax.slice_in_dim(block, 0, width, axis=dim), axis, backward)
        block = jnp.concatenate([low, block, high], axis=dim)
    return block


def from_partner(shard, axis, stride):
    return lax.ppermute(shard, axis, [(i, i ^ 1 << stride) for i in range(lax.axis_size(axis))])


def solve_triangular(matrix, right):
    return jax.scipy.linalg.solve_triangular(matrix, right, lower=True)


def composite(filter_taps):
    count = filter_taps.shape[-1]
    wide = 5 * (count - 1) + 1
    first = jnp.arange(count)[:, None, None]
    second = jnp.arange(count)[None, :, None]
    spot = jnp.arange(wide)[None, None, :]
    table = (first + 4 * second == spot).astype(jnp.float32)
    outer = filter_taps[:, 0, :, None] * filter_taps[:, 1, None, :]
    return jnp.einsum("dab,abm->dm", outer, table, precision=lax.Precision.HIGHEST).astype(
        jnp.bfloat16
    )


def toeplitz(line_taps, length):
    wide = line_taps.shape[0]
    columns = length + wide - 1
    pattern = jnp.concatenate([line_taps, jnp.zeros((length,), line_taps.dtype)])
    return jnp.tile(pattern, length)[: length * columns].reshape(length, columns)


def factor(gram, keep_mask):
    outer = keep_mask[..., :, None] * keep_mask[..., None, :]
    masked = gram * outer
    trace_sum = jnp.sum(jnp.diagonal(masked, axis1=-2, axis2=-1), axis=-1)
    delta = 0.01 * trace_sum / jnp.sum(keep_mask, axis=-1)
    ident = jnp.eye(gram.shape[-1], dtype=jnp.float32)
    shifted = (
        masked
        + ident * (1.0 - keep_mask)[..., None, :]
        + delta[..., None, None] * ident * keep_mask[..., None, :]
    )
    return (masked, jnp.linalg.cholesky(shifted))


def products(zeta):
    return jnp.einsum("...kp,...kq->...pq", zeta, zeta, precision=lax.Precision.HIGHEST)


def transfer(lower, keep_mask, child_z):
    right = keep_mask[..., :, None] * jnp.swapaxes(child_z, -1, -2)
    return jnp.swapaxes(solve_triangular(lower, right), -1, -2)


def rank_mask(rank_value, width):
    return (jnp.arange(width) < rank_value[..., None]).astype(jnp.float32)


def climb_level(child_z, own_gram, partner_gram, keep_mask):
    merged = (own_gram + partner_gram) * 0.5
    masked, lower = factor(merged, keep_mask)
    moved = transfer(lower, keep_mask, child_z)
    zeta = solve_triangular(lower, masked)
    return (moved, zeta, products(zeta))


def local(probes, filter_taps, cluster_ranks):
    combined = composite(filter_taps)
    reach = (combined.shape[1] - 1) // 2
    rows, cols, width = probes.shape
    tall = extended(probes, (("tx", 0),), reach)
    middle = jnp.dot(
        toeplitz(combined[0], rows),
        tall.reshape(tall.shape[0], cols * width),
        preferred_element_type=jnp.float32,
    )
    middle = middle.reshape(rows, cols, width).astype(jnp.bfloat16)
    broad = extended(middle, (("ty", 1),), reach)
    sketch = jnp.einsum(
        "yc,xcp->xyp", toeplitz(combined[1], cols), broad, preferred_element_type=jnp.float32
    ).astype(jnp.bfloat16)
    flat = sketch.reshape(rows * cols, width)
    gram = jnp.einsum("np,nq->pq", flat, flat, preferred_element_type=jnp.float32) / (rows * cols)
    row_at = lax.axis_index("tx")
    col_at = lax.axis_index("ty")
    keep_mask = rank_mask(cluster_ranks[0, row_at, col_at], width)
    masked, lower = factor(gram, keep_mask)
    diag_mask = jnp.eye(width, dtype=jnp.float32) * keep_mask[None, :]
    weights = jnp.swapaxes(solve_triangular(lower, diag_mask), -1, -2).astype(jnp.bfloat16)
    leaf_basis = (
        jnp.dot(flat, weights, preferred_element_type=jnp.float32)
        .astype(jnp.bfloat16)
        .reshape(rows, cols, width)
    )
    zeta = solve_triangular(lower, masked)
    grams = products(zeta)
    row_two = row_at - row_at % 2
    row_four = row_at - row_at % 4
    col_two = col_at - col_at % 2
    col_four = col_at - col_at % 4
    partner = from_partner(grams, "tx", 0)
    first_e, zeta, grams = climb_level(
        zeta, grams, partner, rank_mask(cluster_ranks[1, row_two, col_at], width)
    )
    partner = from_partner(grams, "ty", 0)
    second_e, zeta, grams = climb_level(
        zeta, grams, partner, rank_mask(cluster_ranks[2, row_two, col_two], width)
    )
    partner = from_partner(grams, "tx", 1)
    third_e, zeta, grams = climb_level(
        zeta, grams, partner, rank_mask(cluster_ranks[3, row_four, col_two], width)
    )
    partner = from_partner(grams, "ty", 1)
    fourth_e, zeta, grams = climb_level(
        zeta, grams, partner, rank_mask(cluster_ranks[4, row_four, col_four], width)
    )
    transfers = jnp.stack([first_e, second_e, third_e, fourth_e], axis=0)[None, None]
    return (leaf_basis, transfers)


def solution(mesh):
    in_specs = (P("tx", "ty", None), P(), P())
    out_specs = (P("tx", "ty", None), P("tx", "ty", None, None, None))
    return jax.shard_map(local, mesh=mesh, in_specs=in_specs, out_specs=out_specs, check_vma=False)
```

profile of v0, /device:TPU:140, one launch (start us, length us, event | category | flops | bytes accessed | tf_op | source)
XLA Modules:
  0.0 310.1 jit_solution(15450062606246432339)
XLA Ops:
  0.6 7.0 %fusion.76 = (bf16[80,128,128]{2,1,0:T(8,128)(2,1)}, bf16[80,128,128]{2,1,0:T(8,128)(2,1)}) fusion(bf16[128,128,128]{2,1,0:T(8,128)(2,1)} %param.6), kind=kLoop, calls=%fused_computation.134 | loop fusion | bytes 10485760 | tf_op jit(solution)/shard_map/slice | solution.py:13
  7.7 2.3 collective-permute-start.1
  10.0 3.5 %collective-permute-start = (bf16[80,128,128]{2,1,0:T(8,128)(2,1)}, bf16[80,128,128]{2,1,0:T(8,128)(2,1)}, u32[]{:S(2)}, u32[]{:S(2)}) collective-permute-start(bf16[80,128,128]{2,1,0:T(8,128)(2,1)} %get-tuple-element.12), channel_id=1, source_target_pairs={{0,8},{8,16},{16,24},{24,32},{32,40},{40,48},{48,56},{56,64},{64,7... | collective-permute-start | bytes 7864328 | tf_op jit(solution)/shard_map/ppermute | solution.py:12
  14.8 53.5 %collective-permute-done.1 = bf16[80,128,128]{2,1,0:T(8,128)(2,1)S(1)} collective-permute-done((bf16[80,128,128]{2,1,0:T(8,128)(2,1)}, bf16[80,128,128]{2,1,0:T(8,128)(2,1)S(1)}, u32[]{:S(2)}, u32[]{:S(2)}) %collective-permute-start.1) | collective-permute-done | bytes 2621472 | tf_op jit(solution)/shard_map/ppermute | solution.py:15
  68.4 3.0 collective-permute-done
  71.4 4.3 %pad_maximum_fusion = bf16[288,128,128]{2,1,0:T(8,128)(2,1)S(1)} fusion(bf16[80,128,128]{2,1,0:T(8,128)(2,1)S(1)} %collective-permute-done.1, bf16[128,128,128]{2,1,0:T(8,128)(2,1)} %param.6, bf16[80,128,128]{2,1,0:T(8,128)(2,1)} %collective-permute-done), kind=kLoop, calls=%fused_computation.10 | loop fusion | flops 9437184 | bytes 18874368 | tf_op jit(solution)/shard_map/concatenate | solution.py:16
  75.6 21.2 %fusion.10 = bf16[128,128,128]{2,0,1:T(8,128)(2,1)S(1)} fusion(bf16[128,288]{1,0:T(8,128)(2,1)S(1)} %reshape.135, bf16[36,8,128,128]{3,2,1,0:T(8,128)(2,1)S(1)} %bitcast.157), kind=kOutput, calls=%fused_computation.17 | convolution fusion | flops 1210056704 | bytes 13705216 | tf_op jit(solution)/shard_map/dot_general | solution.py:88
  96.8 3.7 %fusion.75 = (bf16[128,80,128]{2,0,1:T(8,128)(2,1)}, bf16[128,80,128]{2,0,1:T(8,128)(2,1)}) fusion(bf16[128,128,128]{2,0,1:T(8,128)(2,1)S(1)} %fusion.10), kind=kLoop, calls=%fused_computation.133 | loop fusion | bytes 10485760 | tf_op jit(solution)/shard_map/slice | solution.py:13
  100.5 1.9 collective-permute-start.3
  102.4 2.6 collective-permute-start.2
  117.3 14.6 %collective-permute-done.3 = bf16[128,80,128]{2,0,1:T(8,128)(2,1)S(1)} collective-permute-done((bf16[128,80,128]{2,0,1:T(8,128)(2,1)}, bf16[128,80,128]{2,0,1:T(8,128)(2,1)S(1)}, u32[]{:S(2)}, u32[]{:S(2)}) %collective-permute-start.3) | collective-permute-done | bytes 2621472 | tf_op jit(solution)/shard_map/ppermute | solution.py:15
  131.9 3.8 %collective-permute-done.2 = bf16[128,80,128]{2,0,1:T(8,128)(2,1)} collective-permute-done((bf16[128,80,128]{2,0,1:T(8,128)(2,1)}, bf16[128,80,128]{2,0,1:T(8,128)(2,1)}, u32[]{:S(2)}, u32[]{:S(2)}) %collective-permute-start.2) | collective-permute-done | bytes 2621472 | tf_op jit(solution)/shard_map/ppermute | solution.py:12
  135.7 4.1 %pad_maximum_fusion.1 = bf16[128,288,128]{2,0,1:T(8,128)(2,1)S(1)} fusion(bf16[128,80,128]{2,0,1:T(8,128)(2,1)S(1)} %collective-permute-done.3, bf16[128,128,128]{2,0,1:T(8,128)(2,1)} %copy-done, bf16[128,80,128]{2,0,1:T(8,128)(2,1)} %collective-permute-done.2), kind=kLoop, calls=%fused_computation.11 | loop fusion | flops 9437184 | bytes 18874368 | tf_op jit(solution)/shard_map/concatenate | solution.py:16
  139.8 6.5 %fusion.7 = bf16[128,128,128]{1,2,0:T(8,128)(2,1)S(1)} fusion(bf16[128,288,128]{2,0,1:T(8,128)(2,1)S(1)} %pad_maximum_fusion.1, bf16[128,288]{1,0:T(8,128)(2,1)S(1)} %reshape.137), kind=kOutput, calls=%fused_computation.16 | convolution fusion | flops 1210056704 | bytes 13705216 | tf_op jit(solution)/shard_map/yc,xcp->xyp/dot_general | solution.py:95
  146.3 1.9 copy-done.1
  149.7 1.7 gather_fusion
  153.6 11.7 %cholesky.89 = f32[128,128]{1,0:T(8,128)S(1)} custom-call(f32[128,128]{1,0:T(8,128)S(1)} %fusion.54), custom_call_target="Cholesky" | custom-call | tf_op jit(solution)/shard_map/jit(cholesky)/cholesky | solution.py:59
  166.6 9.8 %custom-call.23 = f32[1,128,128]{1,2,0:T(8,128)S(1)} custom-call(f32[1,128,128]{2,1,0:T(8,128)S(1)} %fusion.28), custom_call_target="InvertDiagBlocksLowerTriangular" | custom-call | tf_op jit(solution)/shard_map/jit(_solve_triangular)/triangular_solve | solution.py:25
  177.4 5.2 %collective-permute-start.4 = (f32[128,128]{0,1:T(8,128)S(1)}, f32[128,128]{0,1:T(8,128)S(1)}, u32[]{:S(2)}, u32[]{:S(2)}) collective-permute-start(f32[128,128]{0,1:T(8,128)S(1)} %fusion.78), channel_id=1, source_target_pairs={{0,8},{8,0},{16,24},{24,16},{32,40},{40,32},{48,56},{56,48},{64,72... | collective-permute-start | bytes 196616 | tf_op jit(solution)/shard_map/ppermute | solution.py:21
  182.5 5.5 %convolution_convert_fusion = bf16[16384,128]{1,0:T(8,128)(2,1)} fusion(bf16[16384,128]{1,0:T(8,128)(2,1)} %bitcast.159, bf16[128,128]{1,0:T(8,128)(2,1)S(1)} %convolution_convert_fusion.1), kind=kOutput, calls=%fused_computation.5 | convolution fusion | flops 538968064 | bytes 8421376 | tf_op jit(solution)/shard_map/dot_general | solution.py:107
  191.9 11.7 %cholesky.100 = f32[128,128]{1,0:T(8,128)S(1)} custom-call(f32[128,128]{1,0:T(8,128)S(1)} %fusion.50), custom_call_target="Cholesky" | custom-call | tf_op jit(solution)/shard_map/jit(cholesky)/cholesky | solution.py:59
  204.9 9.8 %custom-call.25 = f32[1,128,128]{1,2,0:T(8,128)S(1)} custom-call(f32[1,128,128]{2,1,0:T(8,128)S(1)} %fusion.29), custom_call_target="InvertDiagBlocksLowerTriangular" | custom-call | tf_op jit(solution)/shard_map/jit(_solve_triangular)/triangular_solve | solution.py:25
  220.5 11.7 %cholesky.111 = f32[128,128]{1,0:T(8,128)S(1)} custom-call(f32[128,128]{1,0:T(8,128)S(1)} %fusion.45), custom_call_target="Cholesky" | custom-call | tf_op jit(solution)/shard_map/jit(cholesky)/cholesky | solution.py:59
  233.6 9.8 %custom-call.27 = f32[1,128,128]{1,2,0:T(8,128)S(1)} custom-call(f32[1,128,128]{2,1,0:T(8,128)S(1)} %fusion.30), custom_call_target="InvertDiagBlocksLowerTriangular" | custom-call | tf_op jit(solution)/shard_map/jit(_solve_triangular)/triangular_solve | solution.py:25
  244.5 5.4 %collective-permute-done.6 = f32[128,128]{0,1:T(8,128)S(1)} collective-permute-done((f32[128,128]{0,1:T(8,128)S(1)}, f32[128,128]{0,1:T(8,128)S(1)}, u32[]{:S(2)}, u32[]{:S(2)}) %collective-permute-start.6) | collective-permute-done | bytes 65568 | tf_op jit(solution)/shard_map/ppermute | solution.py:21
  250.0 1.5 gather_fusion.3
  253.8 11.7 %cholesky.122 = f32[128,128]{1,0:T(8,128)S(1)} custom-call(f32[128,128]{1,0:T(8,128)S(1)} %fusion.40), custom_call_target="Cholesky" | custom-call | tf_op jit(solution)/shard_map/jit(cholesky)/cholesky | solution.py:59
  266.9 9.8 %custom-call.29 = f32[1,128,128]{1,2,0:T(8,128)S(1)} custom-call(f32[1,128,128]{2,1,0:T(8,128)S(1)} %fusion.31), custom_call_target="InvertDiagBlocksLowerTriangular" | custom-call | tf_op jit(solution)/shard_map/jit(_solve_triangular)/triangular_solve | solution.py:25
  279.0 2.8 collective-permute-done.7
  281.8 1.6 gather_fusion.4
  285.7 11.7 %cholesky.133 = f32[128,128]{1,0:T(8,128)S(1)} custom-call(f32[128,128]{1,0:T(8,128)S(1)} %fusion.35), custom_call_target="Cholesky" | custom-call | tf_op jit(solution)/shard_map/jit(cholesky)/cholesky | solution.py:59
  298.8 9.8 %custom-call.31 = f32[1,128,128]{1,2,0:T(8,128)S(1)} custom-call(f32[1,128,128]{2,1,0:T(8,128)S(1)} %fusion.32), custom_call_target="InvertDiagBlocksLowerTriangular" | custom-call | tf_op jit(solution)/shard_map/jit(_solve_triangular)/triangular_solve | solution.py:25
  (100 shorter events, 36.6 us)
Async XLA Ops:
  0.6 12.9 %copy-start.2 = (f32[2,2,33]{2,1,0:T(2,128)S(1)}, f32[2,2,33]{2,1,0:T(2,128)}, u32[]{:S(2)}) copy-start(f32[2,2,33]{2,1,0:T(2,128)} %param.7) | copy-start | bytes 1588
  7.7 60.7 %collective-permute-start.1 = (bf16[80,128,128]{2,1,0:T(8,128)(2,1)}, bf16[80,128,128]{2,1,0:T(8,128)(2,1)S(1)}, u32[]{:S(2)}, u32[]{:S(2)}) collective-permute-start(bf16[80,128,128]{2,1,0:T(8,128)(2,1)} %get-tuple-element.13), channel_id=1, source_target_pairs={{8,0},{16,8},{24,16},{32,24},{40,32},{48,40},{56,48},{64,56},{72,6... | collective-permute-start | bytes 7864328 | tf_op jit(solution)/shard_map/ppermute | solution.py:15
  10.0 61.4 %collective-permute-start = (bf16[80,128,128]{2,1,0:T(8,128)(2,1)}, bf16[80,128,128]{2,1,0:T(8,128)(2,1)}, u32[]{:S(2)}, u32[]{:S(2)}) collective-permute-start(bf16[80,128,128]{2,1,0:T(8,128)(2,1)} %get-tuple-element.12), channel_id=1, source_target_pairs={{0,8},{8,16},{16,24},{24,32},{32,40},{40,48},{48,56},{56,64},{64,7... | collective-permute-start | bytes 7864328 | tf_op jit(solution)/shard_map/ppermute | solution.py:12
  96.8 3.7 %copy-start = (bf16[128,128,128]{2,0,1:T(8,128)(2,1)}, bf16[128,128,128]{2,0,1:T(8,128)(2,1)S(1)}, u32[]{:S(2)}) copy-start(bf16[128,128,128]{2,0,1:T(8,128)(2,1)S(1)} %fusion.10) | copy-start | bytes 12582916
  100.5 31.4 %collective-permute-start.3 = (bf16[128,80,128]{2,0,1:T(8,128)(2,1)}, bf16[128,80,128]{2,0,1:T(8,128)(2,1)S(1)}, u32[]{:S(2)}, u32[]{:S(2)}) collective-permute-start(bf16[128,80,128]{2,0,1:T(8,128)(2,1)} %get-tuple-element.11), channel_id=1, source_target_pairs={{1,0},{2,1},{3,2},{4,3},{5,4},{6,5},{7,6},{9,8},{10,9},{11,10},{12... | collective-permute-start | bytes 7864328 | tf_op jit(solution)/shard_map/ppermute | solution.py:15
  102.4 33.3 %collective-permute-start.2 = (bf16[128,80,128]{2,0,1:T(8,128)(2,1)}, bf16[128,80,128]{2,0,1:T(8,128)(2,1)}, u32[]{:S(2)}, u32[]{:S(2)}) collective-permute-start(bf16[128,80,128]{2,0,1:T(8,128)(2,1)} %get-tuple-element.10), channel_id=1, source_target_pairs={{0,1},{1,2},{2,3},{3,4},{4,5},{5,6},{6,7},{8,9},{9,10},{10,11},{11... | collective-permute-start | bytes 7864328 | tf_op jit(solution)/shard_map/ppermute | solution.py:12
  146.3 1.9 copy-start.1
  177.4 10.7 %collective-permute-start.4 = (f32[128,128]{0,1:T(8,128)S(1)}, f32[128,128]{0,1:T(8,128)S(1)}, u32[]{:S(2)}, u32[]{:S(2)}) collective-permute-start(f32[128,128]{0,1:T(8,128)S(1)} %fusion.78), channel_id=1, source_target_pairs={{0,8},{8,0},{16,24},{24,16},{32,40},{40,32},{48,56},{56,48},{64,72... | collective-permute-start | bytes 196616 | tf_op jit(solution)/shard_map/ppermute | solution.py:21
  215.4 1.3 collective-permute-start.5
  244.1 5.9 %collective-permute-start.6 = (f32[128,128]{0,1:T(8,128)S(1)}, f32[128,128]{0,1:T(8,128)S(1)}, u32[]{:S(2)}, u32[]{:S(2)}) collective-permute-start(f32[128,128]{0,1:T(8,128)S(1)} %fusion.80), channel_id=1, source_target_pairs={{0,16},{8,24},{16,0},{24,8},{32,48},{40,56},{48,32},{56,40},{64,80... | collective-permute-start | bytes 196616 | tf_op jit(solution)/shard_map/ppermute | solution.py:21
  277.4 4.4 %collective-permute-start.7 = (f32[128,128]{0,1:T(8,128)S(1)}, f32[128,128]{0,1:T(8,128)S(1)}, u32[]{:S(2)}, u32[]{:S(2)}) collective-permute-start(f32[128,128]{0,1:T(8,128)S(1)} %fusion.81), channel_id=1, source_target_pairs={{0,2},{1,3},{2,0},{3,1},{4,6},{5,7},{6,4},{7,5},{8,10},{9,11},{10,... | collective-permute-start | bytes 196616 | tf_op jit(solution)/shard_map/ppermute | solution.py:21
where the time goes:
time: 313 us; the launch traced here: 310 us
  other arithmetic  137 us (44%)
  waiting for transfers between devices  84.1 us (27%)
  matrix products  39 us (12%)
  local copies, waits for them, and re-layouts  24.5 us (8%)
  starting transfers between devices  17 us (5%)
  between operations  8.27 us (3%)
    ppermute x2, waiting for transfers between devices, extended(): lax.ppermute(lax.slice_in_dim(block, 0, width, axis=dim), axis, backward)  68.1 us
    another operation x15, other arithmetic, factor(): return (masked, jnp.linalg.cholesky(shifted))  61.9 us
    another operation x10, other arithmetic, solve_triangular(): return jax.scipy.linalg.solve_triangular(matrix, right, lower=True)  52.3 us
    dot_general x1, matrix products, local(): jnp.dot(toeplitz(combined[0], rows), tall.reshape(tall.shape[0], cols * w...  21.2 us
    slice x2, local copies, waits for them, and re-layouts, extended(): lax.slice_in_dim(block, block.shape[dim] - width, None, axis=dim)  10.7 us
    ppermute x4, waiting for transfers between devices, from_partner(): lax.ppermute(shard, axis, [(i, i ^ 1 << stride) for i in range(lax.axis_s...  9.12 us
    concatenate x2, other arithmetic, extended(): block = jnp.concatenate([low, block, high], axis=dim)  8.36 us
    gather x5, local copies, waits for them, and re-layouts, factor(): trace_sum = jnp.sum(jnp.diagonal(masked, axis1=-2, axis2=-1), axis=-1)  7.74 us
  transfers between devices with their start and end apart: 8, of which 7 were waited for; matrix products, arithmetic and copies ran while one was open for 6% of the time, Pallas kernels for 0%

commit v1 on v0

v1 whole, which is shorter than its diff:
```python
import functools

import jax
import jax.numpy as jnp
from jax import lax
from jax.experimental import pallas as pl
from jax.experimental.pallas import tpu as pltpu
from jax.sharding import PartitionSpec as P

HIGHEST = lax.Precision.HIGHEST
PANEL = 16


def extended(block, sides, width):
    for axis, dim in sides:
        count = lax.axis_size(axis)
        forward = [(i, i + 1) for i in range(count - 1)]
        backward = [(target, source) for source, target in forward]
        low = lax.ppermute(
            lax.slice_in_dim(block, block.shape[dim] - width, None, axis=dim), axis, forward
        )
        high = lax.ppermute(lax.slice_in_dim(block, 0, width, axis=dim), axis, backward)
        block = jnp.concatenate([low, block, high], axis=dim)
    return block


def from_partner(shard, axis, stride):
    return lax.ppermute(shard, axis, [(i, i ^ 1 << stride) for i in range(lax.axis_size(axis))])


def composite(filter_taps):
    count = filter_taps.shape[-1]
    wide = 5 * (count - 1) + 1
    first = jnp.arange(count)[:, None, None]
    second = jnp.arange(count)[None, :, None]
    spot = jnp.arange(wide)[None, None, :]
    table = (first + 4 * second == spot).astype(jnp.float32)
    outer = filter_taps[:, 0, :, None] * filter_taps[:, 1, None, :]
    return jnp.einsum("dab,abm->dm", outer, table, precision=HIGHEST).astype(jnp.bfloat16)


def toeplitz(line_taps, length):
    wide = line_taps.shape[0]
    columns = length + wide - 1
    pattern = jnp.concatenate([line_taps, jnp.zeros((length,), line_taps.dtype)])
    return jnp.tile(pattern, length)[: length * columns].reshape(length, columns)


def eliminate(work, size):
    at_row = lax.broadcasted_iota(jnp.int32, (PANEL, size), 0)
    for start in range(0, size, PANEL):
        left = work[pl.ds(start, PANEL), pl.ds(0, size)]
        right = work[pl.ds(start, PANEL), pl.ds(size, size)]
        columns = [
            jnp.broadcast_to(left[:, start + j : start + j + 1], (PANEL, size))
            for j in range(PANEL)
        ]
        scale = jnp.zeros((PANEL, size), jnp.float32)
        for j in range(PANEL):
            pivot = columns[j][j : j + 1, :]
            below = jnp.where(at_row > j, columns[j] * (1.0 / pivot), 0.0)
            for k in range(j + 1, PANEL):
                columns[k] = columns[k] - below * columns[k][j : j + 1, :]
            left = left - below * left[j : j + 1, :]
            right = right - below * right[j : j + 1, :]
            scale = jnp.where(at_row == j, lax.rsqrt(pivot), scale)
        left = left * scale
        right = right * scale
        work[pl.ds(start, PANEL), pl.ds(size, size)] = right
        rest = size - start - PANEL
        if rest:
            tall = left.T[start + PANEL :, :]
            both = jnp.concatenate([left, right], axis=1)
            below = pl.ds(start + PANEL, rest)
            work[below, :] = work[below, :] - jnp.dot(
                tall, both, precision=HIGHEST, preferred_element_type=jnp.float32
            )


def factor_kernel(grams, scale, rank_ref, *refs):
    gram_refs = refs[:grams]
    inverse_ref, zeta_ref, product_ref, work = refs[grams:]
    size = inverse_ref.shape[0]
    rank = rank_ref[0]
    row = lax.broadcasted_iota(jnp.int32, (size, size), 0)
    col = lax.broadcasted_iota(jnp.int32, (size, size), 1)
    gram = gram_refs[0][...]
    for other in gram_refs[1:]:
        gram = gram + other[...]
    masked = jnp.where((row < rank) & (col < rank), gram * scale, 0.0)
    on_diagonal = row == col
    trace = jnp.sum(
        jnp.sum(jnp.where(on_diagonal, masked, 0.0), axis=0, keepdims=True), axis=1, keepdims=True
    )
    delta = 0.01 * trace / rank.astype(jnp.float32)
    shift = jnp.where(row < rank, jnp.broadcast_to(delta, (size, size)), 1.0)
    work[:, pl.ds(0, size)] = masked + jnp.where(on_diagonal, shift, 0.0)
    work[:, pl.ds(size, size)] = jnp.where(on_diagonal, 1.0, 0.0)
    eliminate(work, size)
    inverse = work[:, pl.ds(size, size)]
    zeta = jnp.dot(inverse, masked, precision=HIGHEST, preferred_element_type=jnp.float32)
    zeta_ref[...] = zeta
    product_ref[...] = lax.dot_general(
        zeta,
        zeta,
        (((0,), (0,)), ((), ())),
        precision=HIGHEST,
        preferred_element_type=jnp.float32,
    )
    inverse_ref[...] = jnp.where(col < rank, inverse, 0.0)


def factor(grams, scale, rank):
    size = grams[0].shape[0]
    square = jax.ShapeDtypeStruct((size, size), jnp.float32)
    whole = pl.BlockSpec(memory_space=pltpu.VMEM)
    return pl.pallas_call(
        functools.partial(factor_kernel, len(grams), scale),
        out_shape=(square,) * 3,
        in_specs=[pl.BlockSpec(memory_space=pltpu.SMEM)] + [whole] * len(grams),
        out_specs=(whole,) * 3,
        scratch_shapes=[pltpu.VMEM((size, 2 * size), jnp.float32)],
        compiler_params=pltpu.CompilerParams(vmem_limit_bytes=8 << 20),
        name="factor",
    )(rank.reshape(1), *grams)


def transfer(inverse, child_z):
    return jnp.einsum("qk,pk->qp", child_z, inverse, precision=HIGHEST)


def local(probes, filter_taps, cluster_ranks):
    combined = composite(filter_taps)
    reach = (combined.shape[1] - 1) // 2
    rows, cols, width = probes.shape
    row_at = lax.axis_index("tx")
    col_at = lax.axis_index("ty")
    tall = extended(probes, (("tx", 0),), reach)
    middle = jnp.dot(
        toeplitz(combined[0], rows),
        tall.reshape(tall.shape[0], cols * width),
        preferred_element_type=jnp.float32,
    )
    middle = middle.reshape(rows, cols, width).astype(jnp.bfloat16)
    broad = extended(middle, (("ty", 1),), reach)
    sketch = jnp.einsum(
        "yc,xcp->xyp", toeplitz(combined[1], cols), broad, preferred_element_type=jnp.float32
    ).astype(jnp.bfloat16)
    flat = sketch.reshape(rows * cols, width)
    gram = jnp.einsum("np,nq->pq", flat, flat, preferred_element_type=jnp.float32)
    inverse, zeta, product = factor((gram,), 1.0 / (rows * cols), cluster_ranks[0, row_at, col_at])
    moved = []
    span = {"tx": 1, "ty": 1}
    for level in range(1, cluster_ranks.shape[0]):
        axis = "tx" if level % 2 else "ty"
        partner = from_partner(product, axis, span[axis].bit_length() - 1)
        span[axis] *= 2
        rank = cluster_ranks[
            level, row_at - row_at % span["tx"], col_at - col_at % span["ty"]
        ]
        if level == 1:
            leaf_basis = (
                jnp.dot(flat, inverse.T.astype(jnp.bfloat16), preferred_element_type=jnp.float32)
                .astype(jnp.bfloat16)
                .reshape(rows, cols, width)
            )
        child_z = zeta
        inverse, zeta, product = factor((product, partner), 0.5, rank)
        moved.append(transfer(inverse, child_z))
    return (leaf_basis, jnp.stack(moved, axis=0)[None, None])


def solution(mesh):
    in_specs = (P("tx", "ty", None), P(), P())
    out_specs = (P("tx", "ty", None), P("tx", "ty", None, None, None))
    return jax.shard_map(local, mesh=mesh, in_specs=in_specs, out_specs=out_specs, check_vma=False)
```

time: 313 us -> 201 us (0.64)
  other arithmetic: 137 us -> 9.1 us
  Pallas kernels: 0 us -> 28.5 us
  local copies, waits for them, and re-layouts: 24.5 us -> 13.2 us
  waiting for transfers between devices: 84.1 us -> 94.5 us
  between operations: 8.27 us -> 1.11 us
  matrix products: 39 us -> 34 us
    another operation x25 -> x0, other arithmetic: 114 us -> none  [the longest x15 61.9 us: factor(): return (masked, jnp.linalg.cholesky(shifted))]
    pallas_call x0 -> x5, Pallas kernels: none -> 28.5 us  [factor(): pl.pallas_call(functools.partial(factor_kernel, len(grams), scale), out_s...]
    ppermute x2, waiting for transfers between devices: 68.1 us -> 78.4 us  [extended(): lax.ppermute(lax.slice_in_dim(block, 0, width, axis=dim), axis, backward)]
    gather x5 -> x0, local copies, waits for them, and re-layouts: 7.74 us -> none  [factor(): trace_sum = jnp.sum(jnp.diagonal(masked, axis1=-2, axis2=-1), axis=-1)]
    sub x5 -> x0, other arithmetic: 5.71 us -> none  [factor(): 1.0 - keep_mask]
    reduce_sum x6 -> x0, other arithmetic: 4.29 us -> none  [the longest x5 3.01 us: factor(): trace_sum = jnp.sum(jnp.diagonal(masked, axis1=-2, axis2=-1), axis=-1)]
    convert_element_type x5 -> x0, other arithmetic: 3.19 us -> none  [rank_mask(): return (jnp.arange(width) < rank_value[..., None]).astype(jnp.float32)]
  transfers between devices with their start and end apart: 8 -> 8, of which waited for: 7 -> 7; matrix products, arithmetic and copies ran while one was open for 6% -> 4% of each run, Pallas kernels for 0% -> 0%
where the time goes in v1:
time: 201 us; the launch traced here: 198 us
  waiting for transfers between devices  94.5 us (47%)
  matrix products  34 us (17%)
  Pallas kernels  28.5 us (14%)
  starting transfers between devices  17.5 us (9%)
  local copies, waits for them, and re-layouts  13.2 us (7%)
  other arithmetic  9.1 us (5%)
    ppermute x2, waiting for transfers between devices, extended(): lax.ppermute(lax.slice_in_dim(block, 0, width, axis=dim), axis, backward)  78.4 us
    pallas_call x5, Pallas kernels, factor(): pl.pallas_call(functools.partial(factor_kernel, len(grams), scale), out_s...  28.5 us
    dot_general x1, matrix products, local(): jnp.dot(toeplitz(combined[0], rows), tall.reshape(tall.shape[0], cols * w...  21.2 us
    slice x2, local copies, waits for them, and re-layouts, extended(): lax.slice_in_dim(block, block.shape[dim] - width, None, axis=dim)  10.7 us
    ppermute x4, waiting for transfers between devices, from_partner(): lax.ppermute(shard, axis, [(i, i ^ 1 << stride) for i in range(lax.axis_s...  9.27 us
    concatenate x2, other arithmetic, extended(): block = jnp.concatenate([low, block, high], axis=dim)  8.36 us
    ppermute x4, starting transfers between devices, from_partner(): lax.ppermute(shard, axis, [(i, i ^ 1 << stride) for i in range(lax.axis_s...  7.17 us
    ppermute x2, waiting for transfers between devices, extended(): lax.ppermute(lax.slice_in_dim(block, block.shape[dim] - width, None, axis...  6.84 us
  transfers between devices with their start and end apart: 8, of which 7 were waited for; matrix products, arithmetic and copies ran while one was open for 4% of the time, Pallas kernels for 0%

profile of v1, /device:TPU:140, one launch (start us, length us, event | category | flops | bytes accessed | tf_op | source)
XLA Modules:
  0.0 197.9 jit_solution(14223653221831589432)
XLA Ops:
  0.6 7.0 %fusion.27 = (bf16[80,128,128]{2,1,0:T(8,128)(2,1)}, bf16[80,128,128]{2,1,0:T(8,128)(2,1)}) fusion(bf16[128,128,128]{2,1,0:T(8,128)(2,1)} %param.3), kind=kLoop, calls=%fused_computation.40 | loop fusion | bytes 10485760 | tf_op jit(solution)/shard_map/slice | solution.py:20
  7.7 2.3 %collective-permute-start.1 = (bf16[80,128,128]{2,1,0:T(8,128)(2,1)}, bf16[80,128,128]{2,1,0:T(8,128)(2,1)S(1)}, u32[]{:S(2)}, u32[]{:S(2)}) collective-permute-start(bf16[80,128,128]{2,1,0:T(8,128)(2,1)} %get-tuple-element.33), channel_id=1, source_target_pairs={{8,0},{16,8},{24,16},{32,24},{40,32},{48,40},{56,48},{64,56},{72,6... | collective-permute-start | bytes 7864328 | tf_op jit(solution)/shard_map/ppermute | solution.py:22
  10.0 3.5 %collective-permute-start = (bf16[80,128,128]{2,1,0:T(8,128)(2,1)}, bf16[80,128,128]{2,1,0:T(8,128)(2,1)}, u32[]{:S(2)}, u32[]{:S(2)}) collective-permute-start(bf16[80,128,128]{2,1,0:T(8,128)(2,1)} %get-tuple-element.32), channel_id=1, source_target_pairs={{0,8},{8,16},{16,24},{24,32},{32,40},{40,48},{48,56},{56,64},{64,7... | collective-permute-start | bytes 7864328 | tf_op jit(solution)/shard_map/ppermute | solution.py:19
  13.6 0.6 fusion.18
  14.3 0.3 tile.9
  14.8 53.5 %collective-permute-done.1 = bf16[80,128,128]{2,1,0:T(8,128)(2,1)S(1)} collective-permute-done((bf16[80,128,128]{2,1,0:T(8,128)(2,1)}, bf16[80,128,128]{2,1,0:T(8,128)(2,1)S(1)}, u32[]{:S(2)}, u32[]{:S(2)}) %collective-permute-start.1) | collective-permute-done | bytes 2621472 | tf_op jit(solution)/shard_map/ppermute | solution.py:22
  68.4 3.0 %collective-permute-done = bf16[80,128,128]{2,1,0:T(8,128)(2,1)} collective-permute-done((bf16[80,128,128]{2,1,0:T(8,128)(2,1)}, bf16[80,128,128]{2,1,0:T(8,128)(2,1)}, u32[]{:S(2)}, u32[]{:S(2)}) %collective-permute-start) | collective-permute-done | bytes 2621472 | tf_op jit(solution)/shard_map/ppermute | solution.py:19
  71.4 4.3 %pad_maximum_fusion = bf16[288,128,128]{2,1,0:T(8,128)(2,1)S(1)} fusion(bf16[80,128,128]{2,1,0:T(8,128)(2,1)S(1)} %collective-permute-done.1, bf16[128,128,128]{2,1,0:T(8,128)(2,1)} %param.3, bf16[80,128,128]{2,1,0:T(8,128)(2,1)} %collective-permute-done), kind=kLoop, calls=%fused_computation.5 | loop fusion | flops 9437184 | bytes 18874368 | tf_op jit(solution)/shard_map/concatenate | solution.py:23
  75.6 21.2 %fusion.10 = bf16[128,128,128]{2,0,1:T(8,128)(2,1)S(1)} fusion(bf16[128,288]{1,0:T(8,128)(2,1)S(1)} %reshape.52, bf16[36,8,128,128]{3,2,1,0:T(8,128)(2,1)S(1)} %bitcast.61), kind=kOutput, calls=%fused_computation.12 | convolution fusion | flops 1210056704 | bytes 13705216 | tf_op jit(solution)/shard_map/dot_general | solution.py:139
  96.9 3.7 %fusion.26 = (bf16[128,80,128]{2,0,1:T(8,128)(2,1)}, bf16[128,80,128]{2,0,1:T(8,128)(2,1)}) fusion(bf16[128,128,128]{2,0,1:T(8,128)(2,1)S(1)} %fusion.10), kind=kLoop, calls=%fused_computation.39 | loop fusion | bytes 10485760 | tf_op jit(solution)/shard_map/slice | solution.py:20
  100.5 1.9 collective-permute-start.3
  102.5 2.6 %collective-permute-start.2 = (bf16[128,80,128]{2,0,1:T(8,128)(2,1)}, bf16[128,80,128]{2,0,1:T(8,128)(2,1)}, u32[]{:S(2)}, u32[]{:S(2)}) collective-permute-start(bf16[128,80,128]{2,0,1:T(8,128)(2,1)} %get-tuple-element.30), channel_id=1, source_target_pairs={{0,1},{1,2},{2,3},{3,4},{4,5},{5,6},{6,7},{8,9},{9,10},{10,11},{11... | collective-permute-start | bytes 7864328 | tf_op jit(solution)/shard_map/ppermute | solution.py:19
  105.2 0.3 tile.21
  105.7 1.4 constant_dynamic-slice_fusion.4
  107.1 24.8 %collective-permute-done.3 = bf16[128,80,128]{2,0,1:T(8,128)(2,1)S(1)} collective-permute-done((bf16[128,80,128]{2,0,1:T(8,128)(2,1)}, bf16[128,80,128]{2,0,1:T(8,128)(2,1)S(1)}, u32[]{:S(2)}, u32[]{:S(2)}) %collective-permute-start.3) | collective-permute-done | bytes 2621472 | tf_op jit(solution)/shard_map/ppermute | solution.py:22
  131.9 3.8 %collective-permute-done.2 = bf16[128,80,128]{2,0,1:T(8,128)(2,1)} collective-permute-done((bf16[128,80,128]{2,0,1:T(8,128)(2,1)}, bf16[128,80,128]{2,0,1:T(8,128)(2,1)}, u32[]{:S(2)}, u32[]{:S(2)}) %collective-permute-start.2) | collective-permute-done | bytes 2621472 | tf_op jit(solution)/shard_map/ppermute | solution.py:19
  135.7 4.1 %pad_maximum_fusion.1 = bf16[128,288,128]{2,0,1:T(8,128)(2,1)S(1)} fusion(bf16[128,80,128]{2,0,1:T(8,128)(2,1)S(1)} %collective-permute-done.3, bf16[128,128,128]{2,0,1:T(8,128)(2,1)} %copy-done, bf16[128,80,128]{2,0,1:T(8,128)(2,1)} %collective-permute-done.2), kind=kLoop, calls=%fused_computation.6 | loop fusion | flops 9437184 | bytes 18874368 | tf_op jit(solution)/shard_map/concatenate | solution.py:23
  139.9 6.5 %fusion.7 = bf16[128,128,128]{1,2,0:T(8,128)(2,1)S(1)} fusion(bf16[128,288,128]{2,0,1:T(8,128)(2,1)S(1)} %pad_maximum_fusion.1, bf16[128,288]{1,0:T(8,128)(2,1)S(1)} %reshape.54), kind=kOutput, calls=%fused_computation.11 | convolution fusion | flops 1210056704 | bytes 13705216 | tf_op jit(solution)/shard_map/yc,xcp->xyp/dot_general | solution.py:146
  146.4 1.3 fusion.14.refs_0_
  147.7 5.5 %factor.5 = (f32[128,128]{1,0:T(8,128)S(1)}, f32[128,128]{1,0:T(8,128)S(1)}, f32[128,128]{1,0:T(8,128)S(1)}) custom-call(s32[1]{0:T(128)} %bitcast.8.rank_ref, f32[128,128]{1,0:T(8,128)S(1)} %fusion.14.refs_0_), custom_call_target="tpu_custom_call" | custom-call | tf_op jit(solution)/shard_map/factor/pallas_call | solution.py:117
  153.2 5.5 %collective-permute-start.4 = (f32[128,128]{1,0:T(8,128)S(1)}, f32[128,128]{1,0:T(8,128)S(1)}, u32[]{:S(2)}, u32[]{:S(2)}) collective-permute-start(f32[128,128]{1,0:T(8,128)S(1)} %get-tuple-element.17.refs_0_), channel_id=1, source_target_pairs={{0,8},{8,0},{16,24},{24,16},{32,40},{40,32},{48,56},{56,48},{64,72... | collective-permute-start | bytes 196616 | tf_op jit(solution)/shard_map/ppermute | solution.py:28
  158.7 3.3 %convolution_convert_fusion = bf16[16384,128]{1,0:T(8,128)(2,1)} fusion(bf16[16384,128]{1,0:T(8,128)(2,1)S(1)} %bitcast.63, f32[128,128]{1,0:T(8,128)S(1)} %get-tuple-element.15), kind=kOutput, calls=%fused_computation | convolution fusion | flops 538984448 | bytes 8454144 | tf_op jit(solution)/shard_map/dot_general | solution.py:163
  162.0 5.6 %factor.6 = (f32[128,128]{1,0:T(8,128)S(1)}, f32[128,128]{1,0:T(8,128)S(1)}, f32[128,128]{1,0:T(8,128)S(1)}) custom-call(s32[1]{0:T(128)} %bitcast.11.rank_ref, f32[128,128]{1,0:T(8,128)S(1)} %get-tuple-element.17.refs_0_, f32[128,128]{1,0:T(8,128)S(1)} %collective-permute-done.4.refs_1_), custom_call_target="tpu_custom_call" | custom-call | tf_op jit(solution)/shard_map/factor/pallas_call | solution.py:117
  167.7 0.3 convolution_bitcast_fusion.3
  168.0 1.0 collective-permute-done.5.refs_1_
  169.0 5.6 %factor.7 = (f32[128,128]{1,0:T(8,128)S(1)}, f32[128,128]{1,0:T(8,128)S(1)}, f32[128,128]{1,0:T(8,128)S(1)}) custom-call(s32[1]{0:T(128)} %bitcast.13.rank_ref, f32[128,128]{1,0:T(8,128)S(1)} %get-tuple-element.20.refs_0_, f32[128,128]{1,0:T(8,128)S(1)} %collective-permute-done.5.refs_1_), custom_call_target="tpu_custom_call" | custom-call | tf_op jit(solution)/shard_map/factor/pallas_call | solution.py:117
  174.9 5.5 %collective-permute-done.6.refs_1_ = f32[128,128]{1,0:T(8,128)S(1)} collective-permute-done((f32[128,128]{1,0:T(8,128)S(1)}, f32[128,128]{1,0:T(8,128)S(1)}, u32[]{:S(2)}, u32[]{:S(2)}) %collective-permute-start.6) | collective-permute-done | bytes 65568 | tf_op jit(solution)/shard_map/ppermute | solution.py:28
  180.4 5.6 %factor.8 = (f32[128,128]{1,0:T(8,128)S(1)}, f32[128,128]{1,0:T(8,128)S(1)}, f32[128,128]{1,0:T(8,128)S(1)}) custom-call(s32[1]{0:T(128)} %bitcast.15.rank_ref, f32[128,128]{1,0:T(8,128)S(1)} %get-tuple-element.23.refs_0_, f32[128,128]{1,0:T(8,128)S(1)} %collective-permute-done.6.refs_1_), custom_call_target="tpu_custom_call" | custom-call | tf_op jit(solution)/shard_map/factor/pallas_call | solution.py:117
  186.0 1.5 collective-permute-start.7
  187.8 2.8 %collective-permute-done.7.refs_1_ = f32[128,128]{1,0:T(8,128)S(1)} collective-permute-done((f32[128,128]{1,0:T(8,128)S(1)}, f32[128,128]{1,0:T(8,128)S(1)}, u32[]{:S(2)}, u32[]{:S(2)}) %collective-permute-start.7) | collective-permute-done | bytes 65568 | tf_op jit(solution)/shard_map/ppermute | solution.py:28
  190.6 6.2 %factor.9 = (f32[128,128]{1,0:T(8,128)S(1)}, f32[128,128]{1,0:T(8,128)}, f32[128,128]{1,0:T(8,128)}) custom-call(s32[1]{0:T(128)} %bitcast.17.rank_ref, f32[128,128]{1,0:T(8,128)S(1)} %get-tuple-element.26.refs_0_, f32[128,128]{1,0:T(8,128)S(1)} %collective-permute-done.7.refs_1_), custom_call_target="tpu_custom_call" | custom-call | tf_op jit(solution)/shard_map/factor/pallas_call | solution.py:117
  197.0 0.7 maximum_bitcast_fusion
  (23 shorter events, 1.5 us)
Async XLA Ops:
  0.6 12.9 %copy-start.1 = (f32[2,2,33]{2,1,0:T(2,128)S(1)}, f32[2,2,33]{2,1,0:T(2,128)}, u32[]{:S(2)}) copy-start(f32[2,2,33]{2,1,0:T(2,128)} %param.4) | copy-start | bytes 1588
  7.7 60.7 %collective-permute-start.1 = (bf16[80,128,128]{2,1,0:T(8,128)(2,1)}, bf16[80,128,128]{2,1,0:T(8,128)(2,1)S(1)}, u32[]{:S(2)}, u32[]{:S(2)}) collective-permute-start(bf16[80,128,128]{2,1,0:T(8,128)(2,1)} %get-tuple-element.33), channel_id=1, source_target_pairs={{8,0},{16,8},{24,16},{32,24},{40,32},{48,40},{56,48},{64,56},{72,6... | collective-permute-start | bytes 7864328 | tf_op jit(solution)/shard_map/ppermute | solution.py:22
  10.0 61.4 %collective-permute-start = (bf16[80,128,128]{2,1,0:T(8,128)(2,1)}, bf16[80,128,128]{2,1,0:T(8,128)(2,1)}, u32[]{:S(2)}, u32[]{:S(2)}) collective-permute-start(bf16[80,128,128]{2,1,0:T(8,128)(2,1)} %get-tuple-element.32), channel_id=1, source_target_pairs={{0,8},{8,16},{16,24},{24,32},{32,40},{40,48},{48,56},{56,64},{64,7... | collective-permute-start | bytes 7864328 | tf_op jit(solution)/shard_map/ppermute | solution.py:19
  96.8 3.7 %copy-start = (bf16[128,128,128]{2,0,1:T(8,128)(2,1)}, bf16[128,128,128]{2,0,1:T(8,128)(2,1)S(1)}, u32[]{:S(2)}) copy-start(bf16[128,128,128]{2,0,1:T(8,128)(2,1)S(1)} %fusion.10) | copy-start | bytes 12582916
  100.5 31.4 %collective-permute-start.3 = (bf16[128,80,128]{2,0,1:T(8,128)(2,1)}, bf16[128,80,128]{2,0,1:T(8,128)(2,1)S(1)}, u32[]{:S(2)}, u32[]{:S(2)}) collective-permute-start(bf16[128,80,128]{2,0,1:T(8,128)(2,1)} %get-tuple-element.31), channel_id=1, source_target_pairs={{1,0},{2,1},{3,2},{4,3},{5,4},{6,5},{7,6},{9,8},{10,9},{11,10},{12... | collective-permute-start | bytes 7864328 | tf_op jit(solution)/shard_map/ppermute | solution.py:22
  102.5 33.3 %collective-permute-start.2 = (bf16[128,80,128]{2,0,1:T(8,128)(2,1)}, bf16[128,80,128]{2,0,1:T(8,128)(2,1)}, u32[]{:S(2)}, u32[]{:S(2)}) collective-permute-start(bf16[128,80,128]{2,0,1:T(8,128)(2,1)} %get-tuple-element.30), channel_id=1, source_target_pairs={{0,1},{1,2},{2,3},{3,4},{4,5},{5,6},{6,7},{8,9},{9,10},{10,11},{11... | collective-permute-start | bytes 7864328 | tf_op jit(solution)/shard_map/ppermute | solution.py:19
  153.2 8.8 %collective-permute-start.4 = (f32[128,128]{1,0:T(8,128)S(1)}, f32[128,128]{1,0:T(8,128)S(1)}, u32[]{:S(2)}, u32[]{:S(2)}) collective-permute-start(f32[128,128]{1,0:T(8,128)S(1)} %get-tuple-element.17.refs_0_), channel_id=1, source_target_pairs={{0,8},{8,0},{16,24},{24,16},{32,40},{40,32},{48,56},{56,48},{64,72... | collective-permute-start | bytes 196616 | tf_op jit(solution)/shard_map/ppermute | solution.py:28
  167.6 1.3 collective-permute-start.5
  174.6 5.9 %collective-permute-start.6 = (f32[128,128]{1,0:T(8,128)S(1)}, f32[128,128]{1,0:T(8,128)S(1)}, u32[]{:S(2)}, u32[]{:S(2)}) collective-permute-start(f32[128,128]{1,0:T(8,128)S(1)} %get-tuple-element.23.refs_0_), channel_id=1, source_target_pairs={{0,16},{8,24},{16,0},{24,8},{32,48},{40,56},{48,32},{56,40},{64,80... | collective-permute-start | bytes 196616 | tf_op jit(solution)/shard_map/ppermute | solution.py:28
  186.0 4.5 %collective-permute-start.7 = (f32[128,128]{1,0:T(8,128)S(1)}, f32[128,128]{1,0:T(8,128)S(1)}, u32[]{:S(2)}, u32[]{:S(2)}) collective-permute-start(f32[128,128]{1,0:T(8,128)S(1)} %get-tuple-element.26.refs_0_), channel_id=1, source_target_pairs={{0,2},{1,3},{2,0},{3,1},{4,6},{5,7},{6,4},{7,5},{8,10},{9,11},{10,... | collective-permute-start | bytes 196616 | tf_op jit(solution)/shard_map/ppermute | solution.py:28
